TPU v7x, 32 devices: a whole 2x2x4 slice. The times are simulated.
32 devices in a mesh: section: 2 (over y), rows: 4 (over z), heads: 4 (over x, core).
Axes of the slice: x: 2, y: 2, z: 4, core: 2. Of those that a mesh axis runs over, the one named last changes fastest.
Arguments:
- tokens: bfloat16 [2, 2048, 4, 1024], P('section', 'heads', 'rows'), may hold values from -6 to 6
- image_lengths: int32 [2, 4, 6], P(None, 'rows'), may hold values from 64 to 576, as said below
- tile_ranks: int32 [2, 4, 6], P(None, 'rows'), may hold values from 0 to 5, each once within a row
- w_qkv: bfloat16 [1024, 3, 1024], P(None, None, 'heads'), may hold values from -0.1875 to 0.1875
- bias_qv: bfloat16 [2, 1024], P(None, 'heads'), may hold values from -3 to 3
- w_out: bfloat16 [1024, 1024], P('heads'), may hold values from -1.5 to 1.5
- bias_out: bfloat16 [1024], replicated, may hold values from -3 to 3
- w_up: bfloat16 [1024, 4096], P(None, 'heads'), may hold values from -0.1875 to 0.1875
- bias_up: bfloat16 [4096], P('heads'), may hold values from -3 to 3
- w_down: bfloat16 [4096, 1024], P('heads'), may hold values from -0.09375 to 0.09375
- bias_down: bfloat16 [1024], replicated, may hold values from -3 to 3
- ln1_gain: bfloat16 [1024], replicated, may hold values from 0.5 to 1.5
- ln1_bias: bfloat16 [1024], replicated, may hold values from -3 to 3
- ln2_gain: bfloat16 [1024], replicated, may hold values from 0.5 to 1.5
- ln2_bias: bfloat16 [1024], replicated, may hold values from -3 to 3
- grad_out: bfloat16 [2, 2048, 4, 1024], P(None, None, 'rows', ('section', 'heads')), may hold values from -6 to 6
- grad_tap: bfloat16 [2, 2048, 4, 1024], P(None, None, 'rows', ('section', 'heads')), may hold values from -6 to 6
Outputs:
- block_output: bfloat16 [2, 2048, 4, 1024], P(None, None, 'rows', ('section', 'heads'))
- input_tap: bfloat16 [2, 2048, 4, 1024], P(None, None, 'rows', ('section', 'heads'))
- grad_tokens: float32 [2, 2048, 4, 1024], P('section', 'heads', 'rows')
- grad_w_qkv: float32 [1024, 3, 1024], P(None, None, 'heads')
- grad_bias_qv: float32 [2, 1024], P(None, 'heads')
- grad_w_out: float32 [1024, 1024], P('heads')
- grad_bias_out: float32 [1024], replicated
- grad_w_up: float32 [1024, 4096], P(None, 'heads')
- grad_bias_up: float32 [4096], P('heads')
- grad_w_down: float32 [4096, 1024], P('heads')
- grad_bias_down: float32 [1024], replicated
- grad_ln1_gain: float32 [1024], replicated
- grad_ln1_bias: float32 [1024], replicated
- grad_ln2_gain: float32 [1024], replicated
- grad_ln2_bias: float32 [1024], replicated
Inputs may be any that keep to these rules, and one draw needn't show every extreme that they name: `image_lengths`: each row holds the patch counts of the 6 images of one sequence, in packing order, summing to 1920; the remaining positions of the 2048 are padding; every row has an image of exactly 576 patches and one of exactly 64. `tile_ranks`: each row is an ordering of the images 0 to 5: their places in the decoder's order.
All inputs are finite; a program needn't handle non-finite values.
Results may differ from a plain program's by a relative error of at most 0.024.
Values may be sent and summed in bfloat16 or wider, within the bound.
A program may use at most 192 MiB of HBM per device.

v0:
```python
from functools import partial
import jax
import jax.numpy as jnp
from jax import lax
from jax.sharding import PartitionSpec as P

HD = 64
EPSILON = 1e-06
MASKED = -1e30


def layer_norm(values_in, norm_gain, norm_shift):
    average = jnp.mean(values_in, axis=-1, keepdims=True)
    centred = values_in - average
    variance = jnp.mean(centred * centred, axis=-1, keepdims=True)
    return centred * lax.rsqrt(variance + EPSILON) * norm_gain + norm_shift


def gelu_exact(values_in):
    return jax.nn.gelu(values_in, approximate=False)


def image_tables(lengths, tile_order, extent):
    image_ends = jnp.cumsum(lengths)
    image_starts = image_ends - lengths
    earlier = (tile_order[None, :] < tile_order[:, None]).astype(jnp.int32)
    new_starts = jnp.sum(earlier * lengths[None, :], axis=1)
    position = jnp.arange(extent, dtype=jnp.int32)
    segment = jnp.sum((position[:, None] >= image_ends[None, :]).astype(jnp.int32), axis=1)
    inside_new = (position[:, None] >= new_starts[None, :]) & (
        position[:, None] < (new_starts + lengths)[None, :]
    )
    source = position + jnp.sum(jnp.where(inside_new, image_starts - new_starts, 0), axis=1)
    inside_old = segment[:, None] == jnp.arange(lengths.shape[0], dtype=jnp.int32)[None, :]
    target = position + jnp.sum(jnp.where(inside_old, new_starts - image_starts, 0), axis=1)
    return (segment, source, target)


def reorder_pair(first_rows, second_rows, picks):
    extent = picks.shape[-1]
    columns = jnp.arange(extent, dtype=jnp.int32)
    selector = (picks[..., None] == columns).astype(jnp.bfloat16)
    first_out = jnp.einsum(
        "hspq,hqsc->hpsc", selector, first_rows, preferred_element_type=jnp.float32
    )
    second_out = jnp.einsum(
        "hspq,hqsc->hpsc", selector, second_rows, preferred_element_type=jnp.float32
    )
    return (first_out.astype(jnp.bfloat16), second_out.astype(jnp.bfloat16))


def masked_scores(queries, key_seq, segment_rows, segment_seq):
    scores = jnp.einsum(
        "qhd,khd->hqk", queries, key_seq, preferred_element_type=jnp.float32
    ) * HD ** (-0.5)
    allowed = segment_rows[:, None] == segment_seq[None, :]
    return jnp.where(allowed[None], scores, MASKED)


def attend_forward(query_seq, key_seq, value_seq, segment_seq, block_rows):
    extent = query_seq.shape[0]
    block_count = extent // block_rows
    query_blocks = query_seq.reshape((block_count, block_rows) + query_seq.shape[1:])
    segment_blocks = segment_seq.reshape(block_count, block_rows)

    def one_block(block_item):
        queries, segment_rows = block_item
        scores = masked_scores(queries, key_seq, segment_rows, segment_seq)
        row_max = jnp.max(scores, axis=-1, keepdims=True)
        exponent = jnp.exp(scores - row_max)
        row_total = jnp.sum(exponent, axis=-1, keepdims=True)
        attend_prob = (exponent / row_total).astype(jnp.bfloat16)
        mixture = jnp.einsum(
            "hqk,khd->qhd", attend_prob, value_seq, preferred_element_type=jnp.float32
        )
        return (mixture, (row_max + jnp.log(row_total))[..., 0])

    mixture, log_sum = lax.map(one_block, (query_blocks, segment_blocks))
    return (mixture.reshape(query_seq.shape), log_sum)


def attend_backward(query_seq, key_seq, value_seq, segment_seq, log_sum, grad_seq, block_rows):
    extent = query_seq.shape[0]
    block_count = extent // block_rows
    query_blocks = query_seq.reshape((block_count, block_rows) + query_seq.shape[1:])
    grad_blocks = grad_seq.reshape((block_count, block_rows) + grad_seq.shape[1:])
    segment_blocks = segment_seq.reshape(block_count, block_rows)

    def one_block(running, block_item):
        key_acc, value_acc = running
        queries, segment_rows, log_rows, grad_rows = block_item
        scores = masked_scores(queries, key_seq, segment_rows, segment_seq)
        attend_prob = jnp.exp(scores - log_rows[..., None])
        prob_low = attend_prob.astype(jnp.bfloat16)
        grad_prob = jnp.einsum(
            "qhd,khd->hqk", grad_rows, value_seq, preferred_element_type=jnp.float32
        )
        inner = jnp.sum(attend_prob * grad_prob, axis=-1, keepdims=True)
        grad_score = (attend_prob * (grad_prob - inner) * HD ** (-0.5)).astype(jnp.bfloat16)
        grad_query = jnp.einsum(
            "hqk,khd->qhd", grad_score, key_seq, preferred_element_type=jnp.float32
        )
        key_acc = key_acc + jnp.einsum(
            "hqk,qhd->khd", grad_score, queries, preferred_element_type=jnp.float32
        )
        value_acc = value_acc + jnp.einsum(
            "hqk,qhd->khd", prob_low, grad_rows, preferred_element_type=jnp.float32
        )
        return ((key_acc, value_acc), grad_query)

    zero_rows = jnp.zeros(key_seq.shape, jnp.float32)
    (grad_key, grad_value), grad_query = lax.scan(
        one_block, (zero_rows, zero_rows), (query_blocks, segment_blocks, log_sum, grad_blocks)
    )
    return (grad_query.reshape(query_seq.shape), grad_key, grad_value)


def per_device(
    tokens,
    image_lengths,
    tile_ranks,
    w_qkv,
    bias_qv,
    w_out,
    bias_out,
    w_up,
    bias_up,
    w_down,
    bias_down,
    ln1_gain,
    ln1_bias,
    ln2_gain,
    ln2_bias,
    grad_out,
    grad_tap,
):
    own_tokens = tokens[0]
    part_rows = own_tokens.shape[0]
    seq_count = own_tokens.shape[1]
    full_len = part_rows * lax.axis_size("heads")
    block_rows = min(512, full_len)
    section_at = lax.axis_index("section")
    head_at = lax.axis_index("heads")
    halves = image_lengths.shape[0]
    image_count = image_lengths.shape[2]
    flat_lengths = image_lengths.reshape(halves * seq_count, image_count)
    flat_orders = tile_ranks.reshape(halves * seq_count, image_count)
    segments, sources, targets = jax.vmap(partial(image_tables, extent=full_len))(
        flat_lengths, flat_orders
    )
    segments = segments.reshape(halves, seq_count, full_len)
    sources = sources.reshape(halves, seq_count, full_len)
    targets = targets.reshape(halves, seq_count, full_len)
    own_segments = lax.dynamic_index_in_dim(segments, section_at, 0, keepdims=False)
    row_places = head_at * part_rows + jnp.arange(part_rows, dtype=jnp.int32)
    valid_rows = (
        (jnp.take(own_segments, row_places, axis=1) < image_count).astype(jnp.float32).T[:, :, None]
    )
    token_values = own_tokens.astype(jnp.float32)
    normed_one = layer_norm(token_values, ln1_gain, ln1_bias).astype(jnp.bfloat16)
    gathered_one = lax.all_gather(normed_one, "heads", axis=0, tiled=True)
    projected = jnp.einsum("rsd,dck->rsck", gathered_one, w_qkv, preferred_element_type=jnp.float32)
    query_all = (projected[:, :, 0] + bias_qv[0]).astype(jnp.bfloat16)
    key_all = projected[:, :, 1].astype(jnp.bfloat16)
    value_all = (projected[:, :, 2] + bias_qv[1]).astype(jnp.bfloat16)
    head_groups = query_all.shape[2] // HD
    split_shape = (full_len, seq_count, head_groups, HD)
    query_heads = query_all.reshape(split_shape)
    key_heads = key_all.reshape(split_shape)
    value_heads = value_all.reshape(split_shape)
    which = 0
    mixture, log_sum = attend_forward(
        query_heads[:, which],
        key_heads[:, which],
        value_heads[:, which],
        own_segments[which],
        block_rows,
    )
    mixtures = [mixture]
    log_sums = [log_sum]
    attended = (
        jnp.stack(mixtures, axis=1)
        .reshape(full_len, seq_count, head_groups * HD)
        .astype(jnp.bfloat16)
    )
    picked = attended
    attn_sum = (
        lax.psum_scatter(
            jnp.einsum("rsk,kd->rsd", picked, w_out, preferred_element_type=jnp.float32).astype(
                jnp.bfloat16
            ),
            "heads",
            scatter_dimension=0,
            tiled=True,
        ).astype(jnp.float32)
        + bias_out
    )
    after_attn = token_values + attn_sum
    normed_two = layer_norm(after_attn, ln2_gain, ln2_bias).astype(jnp.bfloat16)
    gathered_two = lax.all_gather(normed_two, "heads", axis=0, tiled=True)
    pre_act = (
        jnp.einsum("rsd,df->rsf", gathered_two, w_up, preferred_element_type=jnp.float32) + bias_up
    )
    activated = gelu_exact(pre_act).astype(jnp.bfloat16)
    picked = activated
    mlp_sum = (
        lax.psum_scatter(
            jnp.einsum("rsf,fd->rsd", picked, w_down, preferred_element_type=jnp.float32).astype(
                jnp.bfloat16
            ),
            "heads",
            scatter_dimension=0,
            tiled=True,
        ).astype(jnp.float32)
        + bias_down
    )
    block_out = ((after_attn + mlp_sum) * valid_rows).astype(jnp.bfloat16)
    sent_out, sent_tap = (
        lax.all_to_all(block_out, ("section", "heads"), split_axis=2, concat_axis=0, tiled=True),
        lax.all_to_all(own_tokens, ("section", "heads"), split_axis=2, concat_axis=0, tiled=True),
    )
    decoder_shape = (halves, full_len, seq_count, sent_out.shape[2])
    output_dec, tap_dec = reorder_pair(
        sent_out.reshape(decoder_shape), sent_tap.reshape(decoder_shape), sources
    )
    encoder_shape = (halves * full_len, seq_count, grad_out.shape[3])
    back_out, back_tap = reorder_pair(grad_out, grad_tap, targets)
    grad_block, grad_direct = (
        lax.all_to_all(
            back_out.reshape(encoder_shape),
            ("section", "heads"),
            split_axis=0,
            concat_axis=2,
            tiled=True,
        ),
        lax.all_to_all(
            back_tap.reshape(encoder_shape),
            ("section", "heads"),
            split_axis=0,
            concat_axis=2,
            tiled=True,
        ),
    )
    grad_mlp_full = grad_block.astype(jnp.float32) * valid_rows
    grad_mlp = grad_mlp_full.astype(jnp.bfloat16)
    grad_b_down = jnp.sum(grad_mlp, axis=(0, 1), dtype=jnp.float32)
    grad_mlp_all = lax.all_gather(grad_mlp, "heads", axis=0, tiled=True)
    grad_w_down_part = jnp.einsum(
        "rsf,rsd->fd", activated, grad_mlp_all, preferred_element_type=jnp.float32
    )
    grad_act = jnp.einsum("rsd,fd->rsf", grad_mlp_all, w_down, preferred_element_type=jnp.float32)
    gelu_back = jax.vjp(gelu_exact, pre_act)[1]
    grad_pre = gelu_back(grad_act)[0].astype(jnp.bfloat16)
    grad_w_up_part = jnp.einsum(
        "rsd,rsf->df", gathered_two, grad_pre, preferred_element_type=jnp.float32
    )
    grad_b_up = jnp.sum(grad_pre, axis=(0, 1), dtype=jnp.float32)
    picked = grad_pre
    grad_normed_two = lax.psum_scatter(
        jnp.einsum("rsf,df->rsd", picked, w_up, preferred_element_type=jnp.float32).astype(
            jnp.bfloat16
        ),
        "heads",
        scatter_dimension=0,
        tiled=True,
    ).astype(jnp.float32)
    norm_two_back = jax.vjp(layer_norm, after_attn, ln2_gain, ln2_bias)[1]
    grad_after, grad_gain_two, grad_shift_two = norm_two_back(grad_normed_two)
    grad_after = grad_after + grad_mlp_full
    grad_attn = grad_after.astype(jnp.bfloat16)
    grad_b_out = jnp.sum(grad_attn, axis=(0, 1), dtype=jnp.float32)
    grad_attn_all = lax.all_gather(grad_attn, "heads", axis=0, tiled=True)
    grad_w_out_part = jnp.einsum(
        "rsk,rsd->kd", attended, grad_attn_all, preferred_element_type=jnp.float32
    )
    grad_attended = (
        jnp.einsum("rsd,kd->rsk", grad_attn_all, w_out, preferred_element_type=jnp.float32)
        .astype(jnp.bfloat16)
        .reshape(split_shape)
    )
    which = 0
    grad_query, grad_key, grad_value = attend_backward(
        query_heads[:, which],
        key_heads[:, which],
        value_heads[:, which],
        own_segments[which],
        log_sums[which],
        grad_attended[:, which],
        block_rows,
    )
    query_grads = [grad_query]
    key_grads = [grad_key]
    value_grads = [grad_value]
    flat_shape = (full_len, seq_count, head_groups * HD)
    grad_query_all = jnp.stack(query_grads, axis=1).reshape(flat_shape).astype(jnp.bfloat16)
    grad_key_all = jnp.stack(key_grads, axis=1).reshape(flat_shape).astype(jnp.bfloat16)
    grad_value_all = jnp.stack(value_grads, axis=1).reshape(flat_shape).astype(jnp.bfloat16)
    grad_projected = jnp.stack([grad_query_all, grad_key_all, grad_value_all], axis=2)
    grad_w_qkv_part = jnp.einsum(
        "rsd,rsck->dck", gathered_one, grad_projected, preferred_element_type=jnp.float32
    )
    grad_b_qv = jnp.stack(
        [
            jnp.sum(grad_query_all, axis=(0, 1), dtype=jnp.float32),
            jnp.sum(grad_value_all, axis=(0, 1), dtype=jnp.float32),
        ]
    )
    picked = grad_projected
    grad_normed_one = lax.psum_scatter(
        jnp.einsum("rsck,dck->rsd", picked, w_qkv, preferred_element_type=jnp.float32).astype(
            jnp.bfloat16
        ),
        "heads",
        scatter_dimension=0,
        tiled=True,
    ).astype(jnp.float32)
    norm_one_back = jax.vjp(layer_norm, token_values, ln1_gain, ln1_bias)[1]
    grad_input, grad_gain_one, grad_shift_one = norm_one_back(grad_normed_one)
    grad_tokens = grad_input + grad_after + grad_direct.astype(jnp.float32)
    (
        grad_w_qkv_part,
        grad_b_qv,
        grad_w_out_part,
        grad_b_out,
        grad_gain_one,
        grad_shift_one,
        grad_w_up_part,
        grad_b_up,
        grad_w_down_part,
        grad_b_down,
        grad_gain_two,
        grad_shift_two,
    ) = (
        lax.psum(grad_w_qkv_part.astype(jnp.bfloat16), ("section", "rows")).astype(jnp.float32),
        lax.psum(grad_b_qv.astype(jnp.bfloat16), ("section", "rows")).astype(jnp.float32),
        lax.psum(grad_w_out_part.astype(jnp.bfloat16), ("section", "rows")).astype(jnp.float32),
        lax.psum(grad_b_out.astype(jnp.bfloat16), ("section", "rows")).astype(jnp.float32),
        lax.psum(grad_gain_one, ("section", "rows")).astype(jnp.float32),
        lax.psum(grad_shift_one, ("section", "rows")).astype(jnp.float32),
        lax.psum(grad_w_up_part.astype(jnp.bfloat16), ("section", "rows")).astype(jnp.float32),
        lax.psum(grad_b_up.astype(jnp.bfloat16), ("section", "rows")).astype(jnp.float32),
        lax.psum(grad_w_down_part.astype(jnp.bfloat16), ("section", "rows")).astype(jnp.float32),
        lax.psum(grad_b_down.astype(jnp.bfloat16), ("section", "rows")).astype(jnp.float32),
        lax.psum(grad_gain_two, ("section", "rows")).astype(jnp.float32),
        lax.psum(grad_shift_two, ("section", "rows")).astype(jnp.float32),
    )
    grad_b_out, grad_b_down, grad_gain_one, grad_shift_one, grad_gain_two, grad_shift_two = (
        lax.psum(
            (grad_b_out, grad_b_down, grad_gain_one, grad_shift_one, grad_gain_two, grad_shift_two),
            "heads",
        )
    )
    return (
        output_dec,
        tap_dec,
        grad_tokens[None],
        grad_w_qkv_part,
        grad_b_qv,
        grad_w_out_part,
        grad_b_out,
        grad_w_up_part,
        grad_b_up,
        grad_w_down_part,
        grad_b_down,
        grad_gain_one,
        grad_shift_one,
        grad_gain_two,
        grad_shift_two,
    )


def solution(mesh):
    placed = (
        P("section", "heads", "rows", None),
        P(None, "rows", None),
        P(None, "rows", None),
        P(None, None, "heads"),
        P(None, "heads"),
        P("heads", None),
        P(),
        P(None, "heads"),
        P("heads"),
        P("heads", None),
        P(),
        P(),
        P(),
        P(),
        P(),
        P(None, None, "rows", ("section", "heads")),
        P(None, None, "rows", ("section", "heads")),
    )
    return jax.shard_map(
        per_device,
        mesh=mesh,
        in_specs=placed,
        out_specs=(
            P(None, None, "rows", ("section", "heads")),
            P(None, None, "rows", ("section", "heads")),
            P("section", "heads", "rows", None),
            P(None, None, "heads"),
            P(None, "heads"),
            P("heads", None),
            P(),
            P(None, "heads"),
            P("heads"),
            P("heads", None),
            P(),
            P(),
            P(),
            P(),
            P(),
        ),
        check_vma=False,
    )
```

profile of v0, /device:TPU:0, one launch (start us, length us, event | category | flops | bytes accessed | tf_op | source)
XLA Modules:
  0.0 1077.3 jit_solution(13621030071722300098)
XLA Ops:
  17.5 35.0 %all-gather.5.cloned.1.call-done = bf16[2048,1,1024]{2,0,1:T(8,128)(2,1)} async-done(((bf16[512,1,1024]{2,0,1:T(8,128)(2,1)}), bf16[2048,1,1024]{2,0,1:T(8,128)(2,1)}) %all-gather.5.cloned.1.call-update) | async-done | bytes 4194320 | tf_op jit(solution)/shard_map/all_gather | solution.py:161
  52.5 5.8 fusion.115
  69.9 62.9 %while.27 = (s32[]{:T(128)}, bf16[4,512,4,64]{1,3,2,0:T(8,128)(2,1)}, f32[4,4,512]{2,1,0:T(4,128)}, s32[4,512]{1,0:T(4,128)S(1)}, s32[1,2048]{1,0:T(1,128)S(1)},...) while((s32[]{:T(128)}, ...), condition=%wide.region_7.8_spmd, body=%wide.region_4.7_spmd.sunk | while | flops 1125120000 | bytes 70072528 | solution.py:78
  95.3 5.1 fusion.232
  111.0 5.1 fusion.232
  139.7 44.5 %reduce-scatter.5.cloned.1.call-done = bf16[512,1,1024]{2,0,1:T(8,128)(2,1)} async-done(((bf16[2048,1,1024]{2,0,1:T(8,128)(2,1)}), bf16[512,1,1024]{2,0,1:T(8,128)(2,1)}) %reduce-scatter.5.cloned.1.call-update) | async-done | bytes 1048592 | tf_op jit(solution)/shard_map/reduce_scatter | solution.py:188
  191.5 7.9 fusion.130
  212.9 22.5 %all-to-all-done.2 = bf16[8,2,32768]{2,1,0:T(2,128)(2,1)} async-done(((bf16[8,2,32768]{2,1,0:T(2,128)(2,1)}), bf16[8,2,32768]{2,1,0:T(2,128)(2,1)}, u32[]{:S(2)}, u32[]{:S(2)}) %all-to-all-start.2) | async-done | bytes 1048608 | tf_op jit(solution)/shard_map/all_to_all | solution.py:229
  235.3 5.8 reshape.983
  245.8 25.9 %multiply_convert_fusion.1 = (bf16[2048,1024]{1,0:T(8,128)(2,1)}, f32[2048,1024]{1,0:T(8,128)}, f32[2048,1024]{1,0:T(8,128)}) fusion(f32[1024]{0:T(1024)S(1)} %convert_element_type.441, bf16[1024,1024]{1,0:T(8,128)(2,1)S(1)} %copy-done, bf16[2048,1,1024]{2,0,1:T(8,128)(2,1)} %all-gather.7.cloned.1.call-done), kind=kOutput, calls=%fused_computation.81 | convolution fusion | flops 4433379328 | bytes 27267072 | tf_op jit(solution)/shard_map/rsd,df->rsf/dot_general | solution.py:202
  271.7 7.7 all-gather.9.cloned.1.call-done
  279.4 13.9 %fusion.186 = (bf16[1024]{0:T(1024)(128)(2,1)}, bf16[2048,1024]{1,0:T(8,128)(2,1)S(1)}) fusion(f32[2048,1024]{1,0:T(8,128)} %get-tuple-element.358, bf16[1024,1024]{1,0:T(8,128)(2,1)} %param.30, bf16[2048,1,1024]{2,0,1:T(8,128)(2,1)} %all-gather.9.cloned.1.call-done, f32[2048,1024]{1,0:T(8,128)} %get-tuple-element.369, f32[1024]{0:T(1024)S(1)} %convert_element_type.441), kind=kOutput, calls=%fused_computation.215 | convolution fusion | flops 4328520704 | bytes 27269120 | tf_op jit(solution)/shard_map/rsd,fd->rsf/dot_general | solution.py:251
  295.3 6.1 convert_bitcast_fusion
  303.0 8.8 convert_bitcast_fusion.1
  312.4 33.6 %reduce-scatter.9.cloned.1.call-done = bf16[512,1,1024]{2,0,1:T(8,128)(2,1)} async-done(((bf16[2048,1,1024]{2,0,1:T(8,128)(2,1)}), bf16[512,1,1024]{2,0,1:T(8,128)(2,1)}) %reduce-scatter.9.cloned.1.call-update) | async-done | bytes 1048592 | tf_op jit(solution)/shard_map/reduce_scatter | solution.py:259
  348.0 45.0 %reduce-scatter.7.cloned.1.call-done = bf16[512,1,1024]{2,0,1:T(8,128)(2,1)} async-done(((bf16[2048,1,1024]{2,0,1:T(8,128)(2,1)}), bf16[512,1,1024]{2,0,1:T(8,128)(2,1)}) %reduce-scatter.7.cloned.1.call-update) | async-done | bytes 1048592 | tf_op jit(solution)/shard_map/reduce_scatter | solution.py:207
  400.9 9.5 fusion.150
  410.4 5.8 fusion.147
  416.2 19.3 %all-gather.11.cloned.1.call-done = bf16[2048,1,1024]{2,0,1:T(8,128)(2,1)} async-done(((bf16[512,1,1024]{2,0,1:T(8,128)(2,1)}), bf16[2048,1,1024]{2,0,1:T(8,128)(2,1)}) %all-gather.11.cloned.1.call-update) | async-done | bytes 4194320 | tf_op jit(solution)/shard_map/all_gather | solution.py:272
  445.9 282.8 %while.28 = (s32[]{:T(128)}, f32[2048,4,64]{0,2,1:T(8,128)}, f32[2048,4,64]{0,2,1:T(8,128)}, bf16[4,512,4,64]{1,3,2,0:T(8,128)(2,1)}, bf16[4,512,4,64]{1,3,2,0:T...) while((s32[]{:T(128)}, f32[2048,4,64]{0,2,1:T(8,128)}, ...), condition=%wide.region_20.21_spmd.clone, body=%wide.region_18.20_spmd.clone.sunk | while | flops 2796560384 | bytes 275323104 | solution.py:112
  450.9 6.8 fusion.246
  457.7 8.1 fusion.243
  465.8 24.0 %fusion.247 = bf16[4,512,4,64]{1,3,2,0:T(8,128)(2,1)} fusion(bf16[4,512,4,64]{1,3,2,0:T(8,128)(2,1)} %get-tuple-element.537, s32[]{:T(128)S(6)} %copy.184, bf16[2048,4,64]{0,2,1:T(8,128)(2,1)S(1)} %get-tuple-element.554, f32[4,512,2048]{2,1,0:T(8,128)} %fusion.243, f32[4,512,2048]{2,1,0:T(8,128)} %copy-done.2, ...), kind=kOutput, calls=%fused_computation.42.clone.1 | convolution fusion | flops 583012352 | bytes 70795264 | tf_op jit(solution)/shard_map/while/body/eval_jaxpr/hqk,khd->qhd/dot_general | solution.py:100
  489.8 25.5 %fusion.245 = f32[2048,4,64]{0,2,1:T(8,128)} fusion(f32[4,512,2048]{2,1,0:T(8,128)} %fusion.243, f32[4,512,2048]{2,1,0:T(8,128)} %copy-done.2, f32[4,512]{1,0:T(4,128)S(1)} %dynamic-slice_bitcast_fusion.2, pred[512,2048]{1,0:T(8,128)(4,1)S(1)} %broadcast_compare_fusion.5, f32[2048,4,64]{0,2,1:T(8,128)} %get-tuple-element.535, pred[]{:T(512)S(6)} %compare.3, ...), kind=kOutput, calls=%fused_computation.39.clone.1 | convolution fusion | flops 584060928 | bytes 73678856 | tf_op jit(solution)/shard_map/while/body/eval_jaxpr/hqk,qhd->khd/dot_general | solution.py:103
  520.1 8.0 fusion.246
  528.1 8.1 fusion.243
  536.2 24.0 %fusion.247 = bf16[4,512,4,64]{1,3,2,0:T(8,128)(2,1)} fusion(bf16[4,512,4,64]{1,3,2,0:T(8,128)(2,1)} %get-tuple-element.537, s32[]{:T(128)S(6)} %copy.184, bf16[2048,4,64]{0,2,1:T(8,128)(2,1)S(1)} %get-tuple-element.554, f32[4,512,2048]{2,1,0:T(8,128)} %fusion.243, f32[4,512,2048]{2,1,0:T(8,128)} %copy-done.2, ...), kind=kOutput, calls=%fused_computation.42.clone.1 | convolution fusion | flops 583012352 | bytes 70795264 | tf_op jit(solution)/shard_map/while/body/eval_jaxpr/hqk,khd->qhd/dot_general | solution.py:100
  560.2 26.1 %fusion.245 = f32[2048,4,64]{0,2,1:T(8,128)} fusion(f32[4,512,2048]{2,1,0:T(8,128)} %fusion.243, f32[4,512,2048]{2,1,0:T(8,128)} %copy-done.2, f32[4,512]{1,0:T(4,128)S(1)} %dynamic-slice_bitcast_fusion.2, pred[512,2048]{1,0:T(8,128)(4,1)S(1)} %broadcast_compare_fusion.5, f32[2048,4,64]{0,2,1:T(8,128)} %get-tuple-element.535, pred[]{:T(512)S(6)} %compare.3, ...), kind=kOutput, calls=%fused_computation.39.clone.1 | convolution fusion | flops 584060928 | bytes 73678856 | tf_op jit(solution)/shard_map/while/body/eval_jaxpr/hqk,qhd->khd/dot_general | solution.py:103
  591.1 8.0 fusion.246
  599.1 8.1 fusion.243
  607.2 24.0 %fusion.247 = bf16[4,512,4,64]{1,3,2,0:T(8,128)(2,1)} fusion(bf16[4,512,4,64]{1,3,2,0:T(8,128)(2,1)} %get-tuple-element.537, s32[]{:T(128)S(6)} %copy.184, bf16[2048,4,64]{0,2,1:T(8,128)(2,1)S(1)} %get-tuple-element.554, f32[4,512,2048]{2,1,0:T(8,128)} %fusion.243, f32[4,512,2048]{2,1,0:T(8,128)} %copy-done.2, ...), kind=kOutput, calls=%fused_computation.42.clone.1 | convolution fusion | flops 583012352 | bytes 70795264 | tf_op jit(solution)/shard_map/while/body/eval_jaxpr/hqk,khd->qhd/dot_general | solution.py:100
  631.2 26.1 %fusion.245 = f32[2048,4,64]{0,2,1:T(8,128)} fusion(f32[4,512,2048]{2,1,0:T(8,128)} %fusion.243, f32[4,512,2048]{2,1,0:T(8,128)} %copy-done.2, f32[4,512]{1,0:T(4,128)S(1)} %dynamic-slice_bitcast_fusion.2, pred[512,2048]{1,0:T(8,128)(4,1)S(1)} %broadcast_compare_fusion.5, f32[2048,4,64]{0,2,1:T(8,128)} %get-tuple-element.535, pred[]{:T(512)S(6)} %compare.3, ...), kind=kOutput, calls=%fused_computation.39.clone.1 | convolution fusion | flops 584060928 | bytes 73678856 | tf_op jit(solution)/shard_map/while/body/eval_jaxpr/hqk,qhd->khd/dot_general | solution.py:103
  662.1 8.0 fusion.246
  670.1 8.1 fusion.243
  678.2 24.0 %fusion.247 = bf16[4,512,4,64]{1,3,2,0:T(8,128)(2,1)} fusion(bf16[4,512,4,64]{1,3,2,0:T(8,128)(2,1)} %get-tuple-element.537, s32[]{:T(128)S(6)} %copy.184, bf16[2048,4,64]{0,2,1:T(8,128)(2,1)S(1)} %get-tuple-element.554, f32[4,512,2048]{2,1,0:T(8,128)} %fusion.243, f32[4,512,2048]{2,1,0:T(8,128)} %copy-done.2, ...), kind=kOutput, calls=%fused_computation.42.clone.1 | convolution fusion | flops 583012352 | bytes 70795264 | tf_op jit(solution)/shard_map/while/body/eval_jaxpr/hqk,khd->qhd/dot_general | solution.py:100
  702.2 26.1 %fusion.245 = f32[2048,4,64]{0,2,1:T(8,128)} fusion(f32[4,512,2048]{2,1,0:T(8,128)} %fusion.243, f32[4,512,2048]{2,1,0:T(8,128)} %copy-done.2, f32[4,512]{1,0:T(4,128)S(1)} %dynamic-slice_bitcast_fusion.2, pred[512,2048]{1,0:T(8,128)(4,1)S(1)} %broadcast_compare_fusion.5, f32[2048,4,64]{0,2,1:T(8,128)} %get-tuple-element.535, pred[]{:T(512)S(6)} %compare.3, ...), kind=kOutput, calls=%fused_computation.39.clone.1 | convolution fusion | flops 584060928 | bytes 73678856 | tf_op jit(solution)/shard_map/while/body/eval_jaxpr/hqk,qhd->khd/dot_general | solution.py:103
  749.0 7.1 fusion.118
  757.3 6.8 fusion.131
  776.3 9.2 reduce.38
  796.2 8.0 reduce.37
  814.3 5.8 reshape.989
  822.8 5.8 reshape.987
  833.6 7.9 fusion.135
  848.3 8.6 fusion.136
  858.6 103.7 %all-reduce.5.cloned.1.call-done = (bf16[1024,3,256]{2,0,1:T(8,128)(2,1)}, bf16[256,1024]{1,0:T(8,128)(2,1)}, bf16[1024,1024]{1,0:T(8,128)(2,1)}, bf16[1024,1024]{1,0:T(8,128)(2,1)}) async-done(((bf16[1024,3,256]{2,0,1:T(8,128)(2,1)}, bf16[256,1024]{1,0:T(8,128)(2,1)}, bf16[1024,1024]{1,0:T(8,128)(2,1)}, bf16[1024,1024]{1,0:T(8,128)(2,1)}), (bf16[1024,3,256]{2,0,1:T(8,128)(2,1)}, ...) | async-done | bytes 6291472 | tf_op jit(solution)/shard_map/psum | solution.py:334
  973.4 35.0 %reduce-scatter.11.cloned.1.call-done = bf16[512,1,1024]{2,0,1:T(8,128)(2,1)} async-done(((bf16[2048,1,1024]{2,0,1:T(8,128)(2,1)}), bf16[512,1,1024]{2,0,1:T(8,128)(2,1)}) %reduce-scatter.11.cloned.1.call-update) | async-done | bytes 1048592 | tf_op jit(solution)/shard_map/reduce_scatter | solution.py:309
  1014.0 37.5 %all-reduce.1 = (bf16[1024]{0:T(1024)(128)(2,1)S(1)}, bf16[1024]{0:T(1024)(128)(2,1)S(1)}, bf16[1024]{0:T(1024)(128)(2,1)S(1)}, bf16[1024]{0:T(1024)(128)(2,1)S(...) all-reduce(bf16[1024]{0:T(1024)(128)(2,1)S(1)} %copy-done.48, ...), channel_id=1, replica_groups=mesh['section'=2,'rows'=4,'heads'=4] {'section','rows'}, use_global_device_ids=true, to_apply=%region_30.31 | all-reduce | flops 7680 | bytes 30720 | tf_op jit(solution)/shard_map/psum | solution.py:337
  1059.4 10.9 %all-reduce = (f32[1024]{0:T(1024)}, f32[1024]{0:T(1024)}, f32[1024]{0:T(1024)}, f32[1024]{0:T(1024)}, f32[1024]{0:T(1024)}, /*index=5*/f32[1024]{0:T(1024)}) all-reduce(bf16[1024]{0:T(1024)(128)(2,1)S(1)} %get-tuple-element.338, ...), channel_id=1, replica_groups=mesh['section'=2,'rows'=4,'heads'=4] {'heads'}, use_global_device_ids=true, to_apply=%region_31.32 | all-reduce | flops 6144 | bytes 36864 | tf_op jit(solution)/shard_map/psum | solution.py:348
  (329 shorter events, 245.0 us)
Async XLA Ops:
  7.2 238.6 %copy-start = (bf16[1024,1024]{1,0:T(8,128)(2,1)S(1)}, bf16[1024,1024]{1,0:T(8,128)(2,1)}, u32[]{:S(2)}) copy-start(bf16[1024,1024]{1,0:T(8,128)(2,1)} %param.28) | copy-start | bytes 6291460
  7.2 8.0 copy-start.51
  7.2 8.2 copy-start.44
  7.2 45.3 %all-gather.5.cloned.1.call-start = ((), (), s32[]{:S(2)}) async-start(), calls=%async_computation.8 | async-start | bytes 5242880 | tf_op jit(solution)/shard_map/all_gather | solution.py:161
  8.8 7.4 copy-start.31
  15.1 169.1 %reduce-scatter.5.cloned.1.call-start = ((), (), s32[]{:S(2)}) async-start(), calls=%async_computation.9 | async-start | bytes 5242880 | tf_op jit(solution)/shard_map/reduce_scatter | solution.py:188
  16.1 36.4 %copy-start.34 = (s32[2,6]{0,1:T(8,128)}, s32[2,6]{0,1:T(8,128)S(1)}, u32[]{:S(2)}) copy-start(s32[2,6]{0,1:T(8,128)S(1)} %reduce_window_sum.11) | copy-start | bytes 148
  16.3 36.2 %copy-start.29 = (s32[2,2048]{1,0:T(2,128)}, s32[2,2048]{1,0:T(2,128)S(1)}, u32[]{:S(2)}) copy-start(s32[2,2048]{1,0:T(2,128)S(1)} %fusion.165) | copy-start | bytes 49156
  139.5 106.2 %all-gather.7.cloned.1.call-start = ((), (), s32[]{:S(2)}) async-start(), calls=%async_computation.10 | async-start | bytes 5242880 | tf_op jit(solution)/shard_map/all_gather | solution.py:200
  139.7 50.4 %copy-start.50 = (s32[2,1,6]{2,1,0:T(1,128)S(1)}, s32[2,1,6]{2,1,0:T(1,128)}, u32[]{:S(2)}) copy-start(s32[2,1,6]{2,1,0:T(1,128)} %param.23) | copy-start | bytes 148
  139.7 50.5 %copy-start.45 = (s32[2,1,6]{2,1,0:T(1,128)S(1)}, s32[2,1,6]{2,1,0:T(1,128)}, u32[]{:S(2)}) copy-start(s32[2,1,6]{2,1,0:T(1,128)} %param.22) | copy-start | bytes 148
  139.7 50.9 %copy-start.35 = (s32[2,6]{0,1:T(8,128)S(1)}, s32[2,6]{0,1:T(8,128)}, u32[]{:S(2)}) copy-start(s32[2,6]{0,1:T(8,128)} %copy-done.34) | copy-start | bytes 148
  139.7 50.9 %copy-start.37 = (s32[2,6]{0,1:T(8,128)S(1)}, s32[2,6]{0,1:T(8,128)}, u32[]{:S(2)}) copy-start(s32[2,6]{0,1:T(8,128)} %copy-done.36) | copy-start | bytes 148
  139.7 50.9 %copy-start.30 = (s32[2,2048]{1,0:T(2,128)S(1)}, s32[2,2048]{1,0:T(2,128)}, u32[]{:S(2)}) copy-start(s32[2,2048]{1,0:T(2,128)} %copy-done.29) | copy-start | bytes 49156
  191.5 7.9 copy-start.42
  205.4 30.0 %all-to-all-start.2 = ((bf16[8,2,32768]{2,1,0:T(2,128)(2,1)}), bf16[8,2,32768]{2,1,0:T(2,128)(2,1)}, u32[]{:S(2)}, u32[]{:S(2)}) async-start(bf16[8,2,32768]{2,1,0:T(2,128)(2,1)} %reshape.982), calls=%async_computation.4 | async-start | bytes 2097152 | tf_op jit(solution)/shard_map/all_to_all | solution.py:229
  209.6 69.8 %all-gather.9.cloned.1.call-start = ((), (), s32[]{:S(2)}) async-start(), calls=%async_computation.12 | async-start | bytes 5242880 | tf_op jit(solution)/shard_map/all_gather | solution.py:247
  212.9 32.9 %copy-start.55 = (bf16[1024]{0:T(1024)(128)(2,1)S(1)}, bf16[1024]{0:T(1024)(128)(2,1)}, u32[]{:S(2)}) copy-start(bf16[1024]{0:T(1024)(128)(2,1)} %param.29) | copy-start | bytes 6148
  245.7 100.4 %reduce-scatter.9.cloned.1.call-start = ((), (), s32[]{:S(2)}) async-start(), calls=%async_computation.13 | async-start | bytes 5242880 | tf_op jit(solution)/shard_map/reduce_scatter | solution.py:259
  301.4 91.6 %reduce-scatter.7.cloned.1.call-start = ((), (), s32[]{:S(2)}) async-start(), calls=%async_computation.11 | async-start | bytes 5242880 | tf_op jit(solution)/shard_map/reduce_scatter | solution.py:207
  311.7 34.3 %copy-start.4 = (bf16[1,512,1,1024]{3,1,2,0:T(8,128)(2,1)S(1)}, bf16[1,512,1,1024]{3,1,2,0:T(8,128)(2,1)}, u32[]{:S(2)}) copy-start(bf16[1,512,1,1024]{3,1,2,0:T(8,128)(2,1)} %param.21) | copy-start | bytes 3145732
  311.7 34.3 %copy-start.7 = (bf16[512,1,1024]{2,0,1:T(8,128)(2,1)S(1)}, bf16[512,1,1024]{2,0,1:T(8,128)(2,1)}, u32[]{:S(2)}) copy-start(bf16[512,1,1024]{2,0,1:T(8,128)(2,1)} %reduce-scatter.5.cloned.1.call-done) | copy-start | bytes 3145732
  311.8 123.7 %all-gather.11.cloned.1.call-start = ((), (), s32[]{:S(2)}) async-start(), calls=%async_computation.14 | async-start | bytes 5242880 | tf_op jit(solution)/shard_map/all_gather | solution.py:272
  400.8 561.5 %all-reduce.5.cloned.1.call-start = ((), (), s32[]{:S(2)}) async-start(), calls=%async_computation.16 | async-start | bytes 12582912 | tf_op jit(solution)/shard_map/psum | solution.py:334
  400.9 9.5 copy-start.59
  400.9 9.5 copy-start.65
  410.4 25.1 %copy-start.63 = (bf16[256,1024]{1,0:T(8,128)(2,1)S(1)}, bf16[256,1024]{1,0:T(8,128)(2,1)}, u32[]{:S(2)}) copy-start(bf16[256,1024]{1,0:T(8,128)(2,1)} %param.26) | copy-start | bytes 1572868
  439.0 7.0 copy-start.9
  520.1 8.1 copy-start.2
  591.1 8.1 copy-start.2
  662.1 8.1 copy-start.2
  747.8 260.6 %reduce-scatter.11.cloned.1.call-start = ((), (), s32[]{:S(2)}) async-start(), calls=%async_computation.15 | async-start | bytes 5242880 | tf_op jit(solution)/shard_map/reduce_scatter | solution.py:309
  764.1 8.3 copy-start.5
  768.0 20.1 %all-to-all-start.3 = ((bf16[8,2,32768]{2,1,0:T(2,128)(2,1)}), bf16[8,2,32768]{2,1,0:T(2,128)(2,1)}, u32[]{:S(2)}, u32[]{:S(2)}) async-start(bf16[8,2,32768]{2,1,0:T(2,128)(2,1)} %reshape.988), calls=%async_computation.7 | async-start | bytes 2097152 | tf_op jit(solution)/shard_map/all_to_all | solution.py:236
  776.3 16.0 %copy-start.16 = (bf16[512,1,1024]{2,0,1:T(8,128)(2,1)S(1)}, bf16[512,1,1024]{2,0,1:T(8,128)(2,1)}, u32[]{:S(2)}) copy-start(bf16[512,1,1024]{2,0,1:T(8,128)(2,1)} %get-tuple-element.365) | copy-start | bytes 3145732
  788.1 22.4 %all-to-all-start.1 = ((bf16[8,2,32768]{2,1,0:T(2,128)(2,1)}), bf16[8,2,32768]{2,1,0:T(2,128)(2,1)}, u32[]{:S(2)}, u32[]{:S(2)}) async-start(bf16[8,2,32768]{2,1,0:T(2,128)(2,1)} %reshape.986), calls=%async_computation.3 | async-start | bytes 2097152 | tf_op jit(solution)/shard_map/all_to_all | solution.py:220
  796.2 18.0 %copy-start.33 = (s32[2,2048]{1,0:T(2,128)S(1)}, s32[2,2048]{1,0:T(2,128)}, u32[]{:S(2)}) copy-start(s32[2,2048]{1,0:T(2,128)} %get-tuple-element.373) | copy-start | bytes 49156
  810.5 31.1 %all-to-all-start = ((bf16[8,2,32768]{2,1,0:T(2,128)(2,1)}), bf16[8,2,32768]{2,1,0:T(2,128)(2,1)S(1)}, u32[]{:S(2)}, u32[]{:S(2)}) async-start(bf16[8,2,32768]{2,1,0:T(2,128)(2,1)} %reshape.984), calls=%async_computation.2 | async-start | bytes 2097152 | tf_op jit(solution)/shard_map/all_to_all | solution.py:219
  970.4 37.9 %copy-start.28 = (f32[1024]{0:T(1024)S(1)}, f32[1024]{0:T(1024)}, u32[]{:S(2)}) copy-start(f32[1024]{0:T(1024)} %copy-done.27) | copy-start | bytes 12292
  970.4 37.9 %copy-start.32 = (f32[512]{0:T(512)S(1)}, f32[512]{0:T(512)}, u32[]{:S(2)}) copy-start(f32[512]{0:T(512)} %copy-done.31) | copy-start | bytes 6148
  970.4 39.7 %copy-start.41 = (f32[512]{0:T(512)S(1)}, f32[512]{0:T(512)}, u32[]{:S(2)}) copy-start(f32[512]{0:T(512)} %copy-done.40) | copy-start | bytes 6148
  970.5 41.1 %copy-start.39 = (f32[512]{0:T(512)S(1)}, f32[512]{0:T(512)}, u32[]{:S(2)}) copy-start(f32[512]{0:T(512)} %copy-done.38) | copy-start | bytes 6148
  973.4 40.6 %copy-start.46 = (bf16[1024]{0:T(1024)(128)(2,1)S(1)}, bf16[1024]{0:T(1024)(128)(2,1)}, u32[]{:S(2)}) copy-start(bf16[1024]{0:T(1024)(128)(2,1)} %get-tuple-element.288) | copy-start | bytes 6148
  973.4 40.6 %copy-start.47 = (bf16[1024]{0:T(1024)(128)(2,1)S(1)}, bf16[1024]{0:T(1024)(128)(2,1)}, u32[]{:S(2)}) copy-start(bf16[1024]{0:T(1024)(128)(2,1)} %get-tuple-element.352) | copy-start | bytes 6148
  973.4 40.6 %copy-start.48 = (bf16[1024]{0:T(1024)(128)(2,1)S(1)}, bf16[1024]{0:T(1024)(128)(2,1)}, u32[]{:S(2)}) copy-start(bf16[1024]{0:T(1024)(128)(2,1)} %get-tuple-element.354) | copy-start | bytes 6148
  973.4 40.6 %copy-start.49 = (bf16[1024]{0:T(1024)(128)(2,1)S(1)}, bf16[1024]{0:T(1024)(128)(2,1)}, u32[]{:S(2)}) copy-start(bf16[1024]{0:T(1024)(128)(2,1)} %get-tuple-element.366) | copy-start | bytes 6148
  973.4 40.6 %copy-start.57 = (bf16[1024]{0:T(1024)(128)(2,1)S(1)}, bf16[1024]{0:T(1024)(128)(2,1)}, u32[]{:S(2)}) copy-start(bf16[1024]{0:T(1024)(128)(2,1)} %get-tuple-element.370) | copy-start | bytes 6148
  1052.1 18.2 %copy-start.1 = (bf16[1024,1024]{1,0:T(8,128)(2,1)S(1)}, bf16[1024,1024]{1,0:T(8,128)(2,1)}, u32[]{:S(2)}) copy-start(bf16[1024,1024]{1,0:T(8,128)(2,1)} %param.28) | copy-start | bytes 6291460
  (46 other events, 145.8 us)
Sparse Core Ops, SparseCore 0:
  15.3 37.1 all-gather.4
  139.7 44.4 reduce-scatter.4
  190.2 44.9 all-gather.6
  245.8 33.5 all-gather.8
  301.5 44.4 reduce-scatter.8
  348.4 44.4 reduce-scatter.6
  401.0 34.4 all-gather.10
  747.9 214.4 all-reduce.4
  964.9 43.4 reduce-scatter.10
where the time goes:
time: 1090 us; the launch traced here: 1080 us
  matrix products  445 us (41%)
  waiting for transfers between devices  351 us (32%)
  other arithmetic  104 us (10%)
  local copies, waits for them, and re-layouts  95.7 us (9%)
  blocking collectives  48.4 us (4%)
  starting transfers between devices  17.1 us (2%)
  between operations  15 us (1%)
    psum x1, waiting for transfers between devices, per_device(): lax.psum(grad_w_qkv_part.astype(jnp.bfloat16), ('section', 'rows'))  104 us
    dot_general x4, matrix products, one_block(): jnp.einsum('hqk,qhd->khd', grad_score, queries, preferred_element_type=jn...  104 us
    dot_general x4, matrix products, one_block(): jnp.einsum('hqk,khd->qhd', grad_score, key_seq, preferred_element_type=jn...  96 us
    unnamed x136, local copies, waits for them, and re-layouts  51.9 us
    reduce_scatter x1, waiting for transfers between devices, per_device(): lax.psum_scatter(jnp.einsum('rsf,fd->rsd', picked, w_down, preferred_elem...  45 us
    reduce_scatter x1, waiting for transfers between devices, per_device(): lax.psum_scatter(jnp.einsum('rsk,kd->rsd', picked, w_out, preferred_eleme...  44.5 us
    psum x1, blocking collectives, per_device(): lax.psum(grad_b_out.astype(jnp.bfloat16), ('section', 'rows'))  37.5 us
    all_gather x1, waiting for transfers between devices, per_device(): gathered_one = lax.all_gather(normed_one, 'heads', axis=0, tiled=True)  35 us
  transfers between devices with their start and end apart: 13, of which 10 were waited for; matrix products, arithmetic and copies ran while one was open for 17% of the time, Pallas kernels for 0%

commit v1 on v0

--- a/solution.py
+++ b/solution.py
@@ -1,12 +1,23 @@
+import functools
 from functools import partial
 import jax
 import jax.numpy as jnp
 from jax import lax
 from jax.sharding import PartitionSpec as P
+from jax.lax import all_to_all, axis_size
 
 HD = 64
 EPSILON = 1e-06
 MASKED = -1e30
+
+
+def views_play(m, which_axis):
+    return jnp.concatenate(
+        all_to_all(jnp.stack(jnp.split(m, axis_size(which_axis), 0)), which_axis, 0, 0), 2
+    )
+
+
+_perform_tails = functools.partial(views_play, which_axis=("section", "heads"))
 
 
 def layer_norm(values_in, norm_gain, norm_shift):
@@ -226,13 +237,7 @@
     encoder_shape = (halves * full_len, seq_count, grad_out.shape[3])
     back_out, back_tap = reorder_pair(grad_out, grad_tap, targets)
     grad_block, grad_direct = (
-        lax.all_to_all(
-            back_out.reshape(encoder_shape),
-            ("section", "heads"),
-            split_axis=0,
-            concat_axis=2,
-            tiled=True,
-        ),
+        _perform_tails(back_out.reshape(encoder_shape)),
         lax.all_to_all(
             back_tap.reshape(encoder_shape),
             ("section", "heads"),

time: 1090 us -> 1080 us (level)
    unnamed x136 -> x138, local copies, waits for them, and re-layouts: 51.9 us -> 48.1 us
  transfers between devices with their start and end apart: 13 -> 13, of which waited for: 10 -> 10; matrix products, arithmetic and copies ran while one was open for 17% -> 16% of each run, Pallas kernels for 0% -> 0%
where the time goes in v1:
time: 1080 us; the launch traced here: 1070 us
  matrix products  444 us (41%)
  waiting for transfers between devices  353 us (33%)
  other arithmetic  103 us (10%)
  local copies, waits for them, and re-layouts  90.3 us (8%)
  blocking collectives  48.4 us (4%)
  starting transfers between devices  17.1 us (2%)
  between operations  15 us (1%)
    dot_general x4, matrix products, one_block(): jnp.einsum('hqk,qhd->khd', grad_score, queries, preferred_element_type=jn...  104 us
    psum x1, waiting for transfers between devices, per_device(): lax.psum(grad_w_qkv_part.astype(jnp.bfloat16), ('section', 'rows'))  104 us
    dot_general x4, matrix products, one_block(): jnp.einsum('hqk,khd->qhd', grad_score, key_seq, preferred_element_type=jn...  96 us
    unnamed x138, local copies, waits for them, and re-layouts  48.1 us
    reduce_scatter x1, waiting for transfers between devices, per_device(): lax.psum_scatter(jnp.einsum('rsf,fd->rsd', picked, w_down, preferred_elem...  45 us
    reduce_scatter x1, waiting for transfers between devices, per_device(): lax.psum_scatter(jnp.einsum('rsk,kd->rsd', picked, w_out, preferred_eleme...  44.5 us
    psum x1, blocking collectives, per_device(): lax.psum(grad_b_out.astype(jnp.bfloat16), ('section', 'rows'))  37.5 us
    all_gather x1, waiting for transfers between devices, per_device(): gathered_one = lax.all_gather(normed_one, 'heads', axis=0, tiled=True)  35 us
  transfers between devices with their start and end apart: 13, of which 10 were waited for; matrix products, arithmetic and copies ran while one was open for 16% of the time, Pallas kernels for 0%

profile of v1, /device:TPU:0, one launch (start us, length us, event | category | flops | bytes accessed | tf_op | source)
XLA Modules:
  0.0 1071.4 jit_solution(9753714632724897030)
XLA Ops:
  17.5 35.0 %all-gather.5.cloned.1.call-done = bf16[2048,1,1024]{2,0,1:T(8,128)(2,1)} async-done(((bf16[512,1,1024]{2,0,1:T(8,128)(2,1)}), bf16[2048,1,1024]{2,0,1:T(8,128)(2,1)}) %all-gather.5.cloned.1.call-update) | async-done | bytes 4194320 | tf_op jit(solution)/shard_map/all_gather | solution.py:172
  52.5 5.8 fusion.115
  69.9 62.9 %while.27 = (s32[]{:T(128)}, bf16[4,512,4,64]{1,3,2,0:T(8,128)(2,1)}, f32[4,4,512]{2,1,0:T(4,128)}, s32[4,512]{1,0:T(4,128)S(1)}, s32[1,2048]{1,0:T(1,128)S(1)},...) while((s32[]{:T(128)}, ...), condition=%wide.region_7.8_spmd, body=%wide.region_4.7_spmd.sunk | while | flops 1125120000 | bytes 70072528 | solution.py:89
  79.6 5.1 fusion.240
  95.2 5.1 fusion.240
  110.9 5.1 fusion.240
  139.7 44.5 %reduce-scatter.5.cloned.1.call-done = bf16[512,1,1024]{2,0,1:T(8,128)(2,1)} async-done(((bf16[2048,1,1024]{2,0,1:T(8,128)(2,1)}), bf16[512,1,1024]{2,0,1:T(8,128)(2,1)}) %reduce-scatter.5.cloned.1.call-update) | async-done | bytes 1048592 | tf_op jit(solution)/shard_map/reduce_scatter | solution.py:199
  191.5 7.1 fusion.130
  211.4 23.7 %all-to-all-done.2 = bf16[8,512,1,128]{3,1,2,0:T(8,128)(2,1)} async-done(((bf16[8,512,1,128]{3,1,2,0:T(8,128)(2,1)}), bf16[8,512,1,128]{3,1,2,0:T(8,128)(2,1)}, u32[]{:S(2)}, u32[]{:S(2)}) %all-to-all-start.2) | async-done | bytes 1048608 | tf_op jit(solution)/shard_map/all_to_all | solution.py:16
  238.3 25.9 %multiply_convert_fusion.1 = (bf16[2048,1024]{1,0:T(8,128)(2,1)}, f32[2048,1024]{1,0:T(8,128)}, f32[2048,1024]{1,0:T(8,128)}) fusion(f32[1024]{0:T(1024)S(1)} %convert_element_type.438, bf16[1024,1024]{1,0:T(8,128)(2,1)S(1)} %copy-done, bf16[2048,1,1024]{2,0,1:T(8,128)(2,1)} %all-gather.7.cloned.1.call-done), kind=kOutput, calls=%fused_computation.81 | convolution fusion | flops 4433379328 | bytes 27267072 | tf_op jit(solution)/shard_map/rsd,df->rsf/dot_general | solution.py:213
  264.2 8.3 all-gather.9.cloned.1.call-done
  272.5 13.9 %fusion.194 = (bf16[1024]{0:T(1024)(128)(2,1)}, bf16[2048,1024]{1,0:T(8,128)(2,1)S(1)}) fusion(f32[2048,1024]{1,0:T(8,128)} %get-tuple-element.358, bf16[1024,1024]{1,0:T(8,128)(2,1)} %param.30, bf16[2048,1,1024]{2,0,1:T(8,128)(2,1)} %all-gather.9.cloned.1.call-done, f32[2048,1024]{1,0:T(8,128)} %get-tuple-element.369, f32[1024]{0:T(1024)S(1)} %convert_element_type.438), kind=kOutput, calls=%fused_computation.231 | convolution fusion | flops 4328520704 | bytes 27269120 | tf_op jit(solution)/shard_map/rsd,fd->rsf/dot_general | solution.py:256
  288.3 6.1 convert_bitcast_fusion
  296.0 8.8 convert_bitcast_fusion.1
  305.5 33.6 %reduce-scatter.9.cloned.1.call-done = bf16[512,1,1024]{2,0,1:T(8,128)(2,1)} async-done(((bf16[2048,1,1024]{2,0,1:T(8,128)(2,1)}), bf16[512,1,1024]{2,0,1:T(8,128)(2,1)}) %reduce-scatter.9.cloned.1.call-update) | async-done | bytes 1048592 | tf_op jit(solution)/shard_map/reduce_scatter | solution.py:264
  341.1 45.0 %reduce-scatter.7.cloned.1.call-done = bf16[512,1,1024]{2,0,1:T(8,128)(2,1)} async-done(((bf16[2048,1,1024]{2,0,1:T(8,128)(2,1)}), bf16[512,1,1024]{2,0,1:T(8,128)(2,1)}) %reduce-scatter.7.cloned.1.call-update) | async-done | bytes 1048592 | tf_op jit(solution)/shard_map/reduce_scatter | solution.py:218
  395.0 9.5 fusion.150
  404.5 5.8 fusion.147
  410.2 19.3 %all-gather.11.cloned.1.call-done = bf16[2048,1,1024]{2,0,1:T(8,128)(2,1)} async-done(((bf16[512,1,1024]{2,0,1:T(8,128)(2,1)}), bf16[2048,1,1024]{2,0,1:T(8,128)(2,1)}) %all-gather.11.cloned.1.call-update) | async-done | bytes 4194320 | tf_op jit(solution)/shard_map/all_gather | solution.py:277
  440.0 282.8 %while.28 = (s32[]{:T(128)}, f32[2048,4,64]{0,2,1:T(8,128)}, f32[2048,4,64]{0,2,1:T(8,128)}, bf16[4,512,4,64]{1,3,2,0:T(8,128)(2,1)}, bf16[4,512,4,64]{1,3,2,0:T...) while((s32[]{:T(128)}, f32[2048,4,64]{0,2,1:T(8,128)}, ...), condition=%wide.region_20.21_spmd.clone, body=%wide.region_18.20_spmd.clone.sunk | while | flops 2796560384 | bytes 275323104 | solution.py:123
  444.9 6.8 fusion.254
  451.7 8.1 fusion.251
  459.8 24.0 %fusion.255 = bf16[4,512,4,64]{1,3,2,0:T(8,128)(2,1)} fusion(bf16[4,512,4,64]{1,3,2,0:T(8,128)(2,1)} %get-tuple-element.537, s32[]{:T(128)S(6)} %copy.191, bf16[2048,4,64]{0,2,1:T(8,128)(2,1)S(1)} %get-tuple-element.554, f32[4,512,2048]{2,1,0:T(8,128)} %fusion.251, f32[4,512,2048]{2,1,0:T(8,128)} %copy-done.2, ...), kind=kOutput, calls=%fused_computation.42.clone.1 | convolution fusion | flops 583012352 | bytes 70795264 | tf_op jit(solution)/shard_map/while/body/eval_jaxpr/hqk,khd->qhd/dot_general | solution.py:111
  483.8 25.5 %fusion.253 = f32[2048,4,64]{0,2,1:T(8,128)} fusion(f32[4,512,2048]{2,1,0:T(8,128)} %fusion.251, f32[4,512,2048]{2,1,0:T(8,128)} %copy-done.2, f32[4,512]{1,0:T(4,128)S(1)} %dynamic-slice_bitcast_fusion.2, pred[512,2048]{1,0:T(8,128)(4,1)S(1)} %broadcast_compare_fusion.5, f32[2048,4,64]{0,2,1:T(8,128)} %get-tuple-element.535, pred[]{:T(512)S(6)} %compare.3, ...), kind=kOutput, calls=%fused_computation.39.clone.1 | convolution fusion | flops 584060928 | bytes 73678856 | tf_op jit(solution)/shard_map/while/body/eval_jaxpr/hqk,qhd->khd/dot_general | solution.py:114
  514.1 8.0 fusion.254
  522.2 8.1 fusion.251
  530.3 24.0 %fusion.255 = bf16[4,512,4,64]{1,3,2,0:T(8,128)(2,1)} fusion(bf16[4,512,4,64]{1,3,2,0:T(8,128)(2,1)} %get-tuple-element.537, s32[]{:T(128)S(6)} %copy.191, bf16[2048,4,64]{0,2,1:T(8,128)(2,1)S(1)} %get-tuple-element.554, f32[4,512,2048]{2,1,0:T(8,128)} %fusion.251, f32[4,512,2048]{2,1,0:T(8,128)} %copy-done.2, ...), kind=kOutput, calls=%fused_computation.42.clone.1 | convolution fusion | flops 583012352 | bytes 70795264 | tf_op jit(solution)/shard_map/while/body/eval_jaxpr/hqk,khd->qhd/dot_general | solution.py:111
  554.2 26.1 %fusion.253 = f32[2048,4,64]{0,2,1:T(8,128)} fusion(f32[4,512,2048]{2,1,0:T(8,128)} %fusion.251, f32[4,512,2048]{2,1,0:T(8,128)} %copy-done.2, f32[4,512]{1,0:T(4,128)S(1)} %dynamic-slice_bitcast_fusion.2, pred[512,2048]{1,0:T(8,128)(4,1)S(1)} %broadcast_compare_fusion.5, f32[2048,4,64]{0,2,1:T(8,128)} %get-tuple-element.535, pred[]{:T(512)S(6)} %compare.3, ...), kind=kOutput, calls=%fused_computation.39.clone.1 | convolution fusion | flops 584060928 | bytes 73678856 | tf_op jit(solution)/shard_map/while/body/eval_jaxpr/hqk,qhd->khd/dot_general | solution.py:114
  585.1 8.0 fusion.254
  593.2 8.1 fusion.251
  601.3 24.0 %fusion.255 = bf16[4,512,4,64]{1,3,2,0:T(8,128)(2,1)} fusion(bf16[4,512,4,64]{1,3,2,0:T(8,128)(2,1)} %get-tuple-element.537, s32[]{:T(128)S(6)} %copy.191, bf16[2048,4,64]{0,2,1:T(8,128)(2,1)S(1)} %get-tuple-element.554, f32[4,512,2048]{2,1,0:T(8,128)} %fusion.251, f32[4,512,2048]{2,1,0:T(8,128)} %copy-done.2, ...), kind=kOutput, calls=%fused_computation.42.clone.1 | convolution fusion | flops 583012352 | bytes 70795264 | tf_op jit(solution)/shard_map/while/body/eval_jaxpr/hqk,khd->qhd/dot_general | solution.py:111
  625.3 26.1 %fusion.253 = f32[2048,4,64]{0,2,1:T(8,128)} fusion(f32[4,512,2048]{2,1,0:T(8,128)} %fusion.251, f32[4,512,2048]{2,1,0:T(8,128)} %copy-done.2, f32[4,512]{1,0:T(4,128)S(1)} %dynamic-slice_bitcast_fusion.2, pred[512,2048]{1,0:T(8,128)(4,1)S(1)} %broadcast_compare_fusion.5, f32[2048,4,64]{0,2,1:T(8,128)} %get-tuple-element.535, pred[]{:T(512)S(6)} %compare.3, ...), kind=kOutput, calls=%fused_computation.39.clone.1 | convolution fusion | flops 584060928 | bytes 73678856 | tf_op jit(solution)/shard_map/while/body/eval_jaxpr/hqk,qhd->khd/dot_general | solution.py:114
  656.2 8.0 fusion.254
  664.2 8.1 fusion.251
  672.3 24.0 %fusion.255 = bf16[4,512,4,64]{1,3,2,0:T(8,128)(2,1)} fusion(bf16[4,512,4,64]{1,3,2,0:T(8,128)(2,1)} %get-tuple-element.537, s32[]{:T(128)S(6)} %copy.191, bf16[2048,4,64]{0,2,1:T(8,128)(2,1)S(1)} %get-tuple-element.554, f32[4,512,2048]{2,1,0:T(8,128)} %fusion.251, f32[4,512,2048]{2,1,0:T(8,128)} %copy-done.2, ...), kind=kOutput, calls=%fused_computation.42.clone.1 | convolution fusion | flops 583012352 | bytes 70795264 | tf_op jit(solution)/shard_map/while/body/eval_jaxpr/hqk,khd->qhd/dot_general | solution.py:111
  696.3 26.1 %fusion.253 = f32[2048,4,64]{0,2,1:T(8,128)} fusion(f32[4,512,2048]{2,1,0:T(8,128)} %fusion.251, f32[4,512,2048]{2,1,0:T(8,128)} %copy-done.2, f32[4,512]{1,0:T(4,128)S(1)} %dynamic-slice_bitcast_fusion.2, pred[512,2048]{1,0:T(8,128)(4,1)S(1)} %broadcast_compare_fusion.5, f32[2048,4,64]{0,2,1:T(8,128)} %get-tuple-element.535, pred[]{:T(512)S(6)} %compare.3, ...), kind=kOutput, calls=%fused_computation.39.clone.1 | convolution fusion | flops 584060928 | bytes 73678856 | tf_op jit(solution)/shard_map/while/body/eval_jaxpr/hqk,qhd->khd/dot_general | solution.py:114
  743.0 7.1 fusion.118
  751.4 6.7 fusion.131
  770.7 9.1 reduce.37
  790.5 8.0 reduce.36
  808.5 5.8 reshape.986
  817.0 5.8 reshape.984
  827.9 7.9 fusion.135
  842.5 8.6 fusion.136
  852.8 103.6 %all-reduce.5.cloned.1.call-done = (bf16[1024,3,256]{2,0,1:T(8,128)(2,1)}, bf16[256,1024]{1,0:T(8,128)(2,1)}, bf16[1024,1024]{1,0:T(8,128)(2,1)}, bf16[1024,1024]{1,0:T(8,128)(2,1)}) async-done(((bf16[1024,3,256]{2,0,1:T(8,128)(2,1)}, bf16[256,1024]{1,0:T(8,128)(2,1)}, bf16[1024,1024]{1,0:T(8,128)(2,1)}, bf16[1024,1024]{1,0:T(8,128)(2,1)}), (bf16[1024,3,256]{2,0,1:T(8,128)(2,1)}, ...) | async-done | bytes 6291472 | tf_op jit(solution)/shard_map/psum | solution.py:339
  967.4 35.0 %reduce-scatter.11.cloned.1.call-done = bf16[512,1,1024]{2,0,1:T(8,128)(2,1)} async-done(((bf16[2048,1,1024]{2,0,1:T(8,128)(2,1)}), bf16[512,1,1024]{2,0,1:T(8,128)(2,1)}) %reduce-scatter.11.cloned.1.call-update) | async-done | bytes 1048592 | tf_op jit(solution)/shard_map/reduce_scatter | solution.py:314
  1008.1 37.5 %all-reduce.1 = (bf16[1024]{0:T(1024)(128)(2,1)S(1)}, bf16[1024]{0:T(1024)(128)(2,1)S(1)}, bf16[1024]{0:T(1024)(128)(2,1)S(1)}, bf16[1024]{0:T(1024)(128)(2,1)S(...) all-reduce(bf16[1024]{0:T(1024)(128)(2,1)S(1)} %copy-done.46, ...), channel_id=1, replica_groups=mesh['section'=2,'rows'=4,'heads'=4] {'section','rows'}, use_global_device_ids=true, to_apply=%region_30.31 | all-reduce | flops 7680 | bytes 30720 | tf_op jit(solution)/shard_map/psum | solution.py:342
  1053.5 10.9 %all-reduce = (f32[1024]{0:T(1024)}, f32[1024]{0:T(1024)}, f32[1024]{0:T(1024)}, f32[1024]{0:T(1024)}, f32[1024]{0:T(1024)}, /*index=5*/f32[1024]{0:T(1024)}) all-reduce(bf16[1024]{0:T(1024)(128)(2,1)S(1)} %get-tuple-element.338, ...), channel_id=1, replica_groups=mesh['section'=2,'rows'=4,'heads'=4] {'heads'}, use_global_device_ids=true, to_apply=%region_31.32 | all-reduce | flops 6144 | bytes 36864 | tf_op jit(solution)/shard_map/psum | solution.py:353
  (329 shorter events, 239.0 us)
Async XLA Ops:
  7.2 231.1 %copy-start = (bf16[1024,1024]{1,0:T(8,128)(2,1)S(1)}, bf16[1024,1024]{1,0:T(8,128)(2,1)}, u32[]{:S(2)}) copy-start(bf16[1024,1024]{1,0:T(8,128)(2,1)} %param.28) | copy-start | bytes 6291460
  7.2 8.0 copy-start.49
  7.2 8.2 copy-start.42
  7.2 45.2 %all-gather.5.cloned.1.call-start = ((), (), s32[]{:S(2)}) async-start(), calls=%async_computation.8 | async-start | bytes 5242880 | tf_op jit(solution)/shard_map/all_gather | solution.py:172
  8.8 7.4 copy-start.29
  15.1 169.0 %reduce-scatter.5.cloned.1.call-start = ((), (), s32[]{:S(2)}) async-start(), calls=%async_computation.9 | async-start | bytes 5242880 | tf_op jit(solution)/shard_map/reduce_scatter | solution.py:199
  16.1 36.4 %copy-start.32 = (s32[2,6]{0,1:T(8,128)}, s32[2,6]{0,1:T(8,128)S(1)}, u32[]{:S(2)}) copy-start(s32[2,6]{0,1:T(8,128)S(1)} %reduce_window_sum.11) | copy-start | bytes 148
  16.2 36.2 %copy-start.27 = (s32[2,2048]{1,0:T(2,128)}, s32[2,2048]{1,0:T(2,128)S(1)}, u32[]{:S(2)}) copy-start(s32[2,2048]{1,0:T(2,128)S(1)} %fusion.173) | copy-start | bytes 49156
  139.5 98.8 %all-gather.7.cloned.1.call-start = ((), (), s32[]{:S(2)}) async-start(), calls=%async_computation.10 | async-start | bytes 5242880 | tf_op jit(solution)/shard_map/all_gather | solution.py:211
  139.6 50.4 %copy-start.48 = (s32[2,1,6]{2,1,0:T(1,128)S(1)}, s32[2,1,6]{2,1,0:T(1,128)}, u32[]{:S(2)}) copy-start(s32[2,1,6]{2,1,0:T(1,128)} %param.23) | copy-start | bytes 148
  139.6 50.5 %copy-start.43 = (s32[2,1,6]{2,1,0:T(1,128)S(1)}, s32[2,1,6]{2,1,0:T(1,128)}, u32[]{:S(2)}) copy-start(s32[2,1,6]{2,1,0:T(1,128)} %param.22) | copy-start | bytes 148
  139.7 50.9 %copy-start.33 = (s32[2,6]{0,1:T(8,128)S(1)}, s32[2,6]{0,1:T(8,128)}, u32[]{:S(2)}) copy-start(s32[2,6]{0,1:T(8,128)} %copy-done.32) | copy-start | bytes 148
  139.7 50.9 %copy-start.35 = (s32[2,6]{0,1:T(8,128)S(1)}, s32[2,6]{0,1:T(8,128)}, u32[]{:S(2)}) copy-start(s32[2,6]{0,1:T(8,128)} %copy-done.34) | copy-start | bytes 148
  139.7 50.9 %copy-start.28 = (s32[2,2048]{1,0:T(2,128)S(1)}, s32[2,2048]{1,0:T(2,128)}, u32[]{:S(2)}) copy-start(s32[2,2048]{1,0:T(2,128)} %copy-done.27) | copy-start | bytes 49156
  191.4 7.1 copy-start.40
  201.2 37.0 %copy-start.53 = (bf16[1024]{0:T(1024)(128)(2,1)S(1)}, bf16[1024]{0:T(1024)(128)(2,1)}, u32[]{:S(2)}) copy-start(bf16[1024]{0:T(1024)(128)(2,1)} %param.29) | copy-start | bytes 6148
  203.9 31.2 %all-to-all-start.2 = ((bf16[8,512,1,128]{3,1,2,0:T(8,128)(2,1)}), bf16[8,512,1,128]{3,1,2,0:T(8,128)(2,1)}, u32[]{:S(2)}, u32[]{:S(2)}) async-start(bf16[8,512,1,128]{3,1,2,0:T(8,128)(2,1)} %fusion.165), calls=%async_computation.4 | async-start | bytes 2097152 | tf_op jit(solution)/shard_map/all_to_all | solution.py:16
  208.2 64.3 %all-gather.9.cloned.1.call-start = ((), (), s32[]{:S(2)}) async-start(), calls=%async_computation.12 | async-start | bytes 5242880 | tf_op jit(solution)/shard_map/all_gather | solution.py:252
  238.2 100.9 %reduce-scatter.9.cloned.1.call-start = ((), (), s32[]{:S(2)}) async-start(), calls=%async_computation.13 | async-start | bytes 5242880 | tf_op jit(solution)/shard_map/reduce_scatter | solution.py:264
  294.4 91.6 %reduce-scatter.7.cloned.1.call-start = ((), (), s32[]{:S(2)}) async-start(), calls=%async_computation.11 | async-start | bytes 5242880 | tf_op jit(solution)/shard_map/reduce_scatter | solution.py:218
  304.8 34.3 %copy-start.4 = (bf16[1,512,1,1024]{3,1,2,0:T(8,128)(2,1)S(1)}, bf16[1,512,1,1024]{3,1,2,0:T(8,128)(2,1)}, u32[]{:S(2)}) copy-start(bf16[1,512,1,1024]{3,1,2,0:T(8,128)(2,1)} %param.21) | copy-start | bytes 3145732
  304.8 34.3 %copy-start.7 = (bf16[512,1,1024]{2,0,1:T(8,128)(2,1)S(1)}, bf16[512,1,1024]{2,0,1:T(8,128)(2,1)}, u32[]{:S(2)}) copy-start(bf16[512,1,1024]{2,0,1:T(8,128)(2,1)} %reduce-scatter.5.cloned.1.call-done) | copy-start | bytes 3145732
  304.8 124.7 %all-gather.11.cloned.1.call-start = ((), (), s32[]{:S(2)}) async-start(), calls=%async_computation.14 | async-start | bytes 5242880 | tf_op jit(solution)/shard_map/all_gather | solution.py:277
  394.9 561.5 %all-reduce.5.cloned.1.call-start = ((), (), s32[]{:S(2)}) async-start(), calls=%async_computation.16 | async-start | bytes 12582912 | tf_op jit(solution)/shard_map/psum | solution.py:339
  395.0 9.5 copy-start.57
  395.0 9.5 copy-start.63
  404.5 25.1 %copy-start.61 = (bf16[256,1024]{1,0:T(8,128)(2,1)S(1)}, bf16[256,1024]{1,0:T(8,128)(2,1)}, u32[]{:S(2)}) copy-start(bf16[256,1024]{1,0:T(8,128)(2,1)} %param.26) | copy-start | bytes 1572868
  433.0 6.9 copy-start.9
  514.1 8.1 copy-start.2
  585.1 8.1 copy-start.2
  656.1 8.1 copy-start.2
  741.8 260.6 %reduce-scatter.11.cloned.1.call-start = ((), (), s32[]{:S(2)}) async-start(), calls=%async_computation.15 | async-start | bytes 5242880 | tf_op jit(solution)/shard_map/reduce_scatter | solution.py:314
  758.1 8.6 copy-start.5
  762.3 20.0 %all-to-all-start.3 = ((bf16[8,2,32768]{2,1,0:T(2,128)(2,1)}), bf16[8,2,32768]{2,1,0:T(2,128)(2,1)}, u32[]{:S(2)}, u32[]{:S(2)}) async-start(bf16[8,2,32768]{2,1,0:T(2,128)(2,1)} %reshape.985), calls=%async_computation.7 | async-start | bytes 2097152 | tf_op jit(solution)/shard_map/all_to_all | solution.py:241
  770.7 16.0 %copy-start.14 = (bf16[512,1,1024]{2,0,1:T(8,128)(2,1)S(1)}, bf16[512,1,1024]{2,0,1:T(8,128)(2,1)}, u32[]{:S(2)}) copy-start(bf16[512,1,1024]{2,0,1:T(8,128)(2,1)} %get-tuple-element.365) | copy-start | bytes 3145732
  782.4 22.3 %all-to-all-start.1 = ((bf16[8,2,32768]{2,1,0:T(2,128)(2,1)}), bf16[8,2,32768]{2,1,0:T(2,128)(2,1)}, u32[]{:S(2)}, u32[]{:S(2)}) async-start(bf16[8,2,32768]{2,1,0:T(2,128)(2,1)} %reshape.983), calls=%async_computation.3 | async-start | bytes 2097152 | tf_op jit(solution)/shard_map/all_to_all | solution.py:231
  790.5 17.9 %copy-start.31 = (s32[2,2048]{1,0:T(2,128)S(1)}, s32[2,2048]{1,0:T(2,128)}, u32[]{:S(2)}) copy-start(s32[2,2048]{1,0:T(2,128)} %get-tuple-element.373) | copy-start | bytes 49156
  804.7 31.1 %all-to-all-start = ((bf16[8,2,32768]{2,1,0:T(2,128)(2,1)}), bf16[8,2,32768]{2,1,0:T(2,128)(2,1)S(1)}, u32[]{:S(2)}, u32[]{:S(2)}) async-start(bf16[8,2,32768]{2,1,0:T(2,128)(2,1)} %reshape.981), calls=%async_computation.2 | async-start | bytes 2097152 | tf_op jit(solution)/shard_map/all_to_all | solution.py:230
  964.5 37.9 %copy-start.26 = (f32[1024]{0:T(1024)S(1)}, f32[1024]{0:T(1024)}, u32[]{:S(2)}) copy-start(f32[1024]{0:T(1024)} %copy-done.25) | copy-start | bytes 12292
  964.5 37.9 %copy-start.30 = (f32[512]{0:T(512)S(1)}, f32[512]{0:T(512)}, u32[]{:S(2)}) copy-start(f32[512]{0:T(512)} %copy-done.29) | copy-start | bytes 6148
  964.5 39.7 %copy-start.39 = (f32[512]{0:T(512)S(1)}, f32[512]{0:T(512)}, u32[]{:S(2)}) copy-start(f32[512]{0:T(512)} %copy-done.38) | copy-start | bytes 6148
  964.5 41.1 %copy-start.37 = (f32[512]{0:T(512)S(1)}, f32[512]{0:T(512)}, u32[]{:S(2)}) copy-start(f32[512]{0:T(512)} %copy-done.36) | copy-start | bytes 6148
  967.4 40.6 %copy-start.44 = (bf16[1024]{0:T(1024)(128)(2,1)S(1)}, bf16[1024]{0:T(1024)(128)(2,1)}, u32[]{:S(2)}) copy-start(bf16[1024]{0:T(1024)(128)(2,1)} %get-tuple-element.288) | copy-start | bytes 6148
  967.4 40.6 %copy-start.45 = (bf16[1024]{0:T(1024)(128)(2,1)S(1)}, bf16[1024]{0:T(1024)(128)(2,1)}, u32[]{:S(2)}) copy-start(bf16[1024]{0:T(1024)(128)(2,1)} %get-tuple-element.352) | copy-start | bytes 6148
  967.4 40.6 %copy-start.46 = (bf16[1024]{0:T(1024)(128)(2,1)S(1)}, bf16[1024]{0:T(1024)(128)(2,1)}, u32[]{:S(2)}) copy-start(bf16[1024]{0:T(1024)(128)(2,1)} %get-tuple-element.354) | copy-start | bytes 6148
  967.4 40.6 %copy-start.47 = (bf16[1024]{0:T(1024)(128)(2,1)S(1)}, bf16[1024]{0:T(1024)(128)(2,1)}, u32[]{:S(2)}) copy-start(bf16[1024]{0:T(1024)(128)(2,1)} %get-tuple-element.366) | copy-start | bytes 6148
  967.4 40.6 %copy-start.55 = (bf16[1024]{0:T(1024)(128)(2,1)S(1)}, bf16[1024]{0:T(1024)(128)(2,1)}, u32[]{:S(2)}) copy-start(bf16[1024]{0:T(1024)(128)(2,1)} %get-tuple-element.370) | copy-start | bytes 6148
  1046.2 18.2 %copy-start.1 = (bf16[1024,1024]{1,0:T(8,128)(2,1)S(1)}, bf16[1024,1024]{1,0:T(8,128)(2,1)}, u32[]{:S(2)}) copy-start(bf16[1024,1024]{1,0:T(8,128)(2,1)} %param.28) | copy-start | bytes 6291460
  (44 other events, 140.1 us)
Sparse Core Ops, SparseCore 0:
  15.2 37.1 all-gather.4
  139.6 44.4 reduce-scatter.4
  190.1 45.7 all-gather.6
  238.3 34.1 all-gather.8
  294.6 44.5 reduce-scatter.8
  341.5 44.4 reduce-scatter.6
  395.0 34.4 all-gather.10
  741.9 214.4 all-reduce.4
  958.9 43.4 reduce-scatter.10
